TPU v7x, 256 devices: a whole 4x4x8 slice. The times are simulated.
256 devices in a mesh: seq: 32 (over z_hi, x, y), head: 8 (over z_lo, core).
Axes of the slice: x: 4, y: 4, z: 8 (z_hi: 2, z_lo: 4; z = z_hi * 4 + z_lo), core: 2. Of those that a mesh axis runs over, the one named last changes fastest.
Arguments:
- queries: bfloat16 [8192, 64, 192], P('seq', 'head'), may hold values from -50 to 50
- grad_out: bfloat16 [8192, 64, 128], P('seq', 'head'), may hold values from -6 to 6
- latent: bfloat16 [8192, 576], P('seq'), may hold values from -18 to 18
- w_uk: bfloat16 [64, 512, 128], P('head'), may hold values from -0.25 to 0.25
- w_uv: bfloat16 [64, 512, 128], P('head'), may hold values from -0.25 to 0.25
- doc_start: int32 [8192], P('seq'), may hold values from 0 to 8191, as said below
Outputs:
- grad_query: bfloat16 [8192, 64, 192], P('seq', 'head')
- grad_latent: float32 [8192, 576], P(('seq', 'head'))
Inputs may be any that keep to these rules, and one draw needn't show every extreme that they name: doc_start[t] is the first position of the document that holds position t; documents follow one another, each of 1 to 768 positions, and one is exactly 768 long.
All inputs are finite; a program needn't handle non-finite values.
Results may differ from a plain program's by a relative error of at most 0.008.
Values may be sent and summed in bfloat16 or wider, within the bound.
No kernel may reach another device: no remote copies, remote signals or barrier semaphores. Data moves between devices by JAX's collectives and lax.ppermute only.
A program may use at most 64 MiB of HBM per device.

v0:
```python
import functools
import math

import jax
import jax.numpy as jnp
from jax import lax
from jax.experimental import pallas as pl
from jax.experimental.pallas import tpu as pltpu
from jax.sharding import PartitionSpec as P

BACK = 3
CORES = 2
BF16 = jnp.bfloat16
F32 = jnp.float32


def dot(a, b, contract=((1,), (0,))):
    return lax.dot_general(a, b, (contract, ((), ())), preferred_element_type=F32)


LOWEST = -1e30


def prepare_kernel(
    info_ref, qt_ref, gt_ref, uk_ref, uv_ref, start_ref,
    qct_ref, qc_ref, glt_ref, gl_ref, bias_ref,
):
    pair, latw, nope = uk_ref.shape
    tokens = qt_ref.shape[2]
    for n in range(pair):
        uk, uv = uk_ref[n], uv_ref[n]
        rows = slice(n * tokens, (n + 1) * tokens)
        qct_ref[n, :latw] = dot(uk, qt_ref[n, :nope]).astype(BF16)
        qct_ref[n, latw:] = qt_ref[n, nope:]
        qc_ref[rows, :latw] = dot(qt_ref[n, :nope].T, uk, ((1,), (1,))).astype(BF16)
        qc_ref[rows, latw:] = qt_ref[n, nope:].T
        glt_ref[n] = dot(uv, gt_ref[n]).astype(BF16)
        gl_ref[rows] = dot(gt_ref[n].T, uv, ((1,), (1,))).astype(BF16)
    shape = bias_ref.shape
    row = pl.program_id(0) * shape[0] + lax.broadcasted_iota(jnp.int32, shape, 0)
    kpos = info_ref[1] + row
    qpos = info_ref[1] + BACK * tokens + lax.broadcasted_iota(jnp.int32, shape, 1)
    visible = (kpos >= start_ref[...]) & (kpos <= qpos)
    bias_ref[...] = jnp.where(visible, 0.0, -jnp.inf).astype(F32)


def prepare(info, qt, gt, w_uk, w_uv, doc_start, pair=2):
    heads, qw, tokens = qt.shape
    latw, nope = w_uk.shape[1:]
    vdim = gt.shape[1]
    width = latw + qw - nope
    span = (BACK + 1) * tokens
    one = lambda *dims: pl.BlockSpec((pair, *dims), lambda h, s: (h, 0, 0))
    rows = lambda n, d: pl.BlockSpec((pair * n, d), lambda h, s: (h, 0))
    return pl.pallas_call(
        prepare_kernel,
        out_shape=(
            jax.ShapeDtypeStruct((heads, width, tokens), BF16),
            jax.ShapeDtypeStruct((heads * tokens, width), BF16),
            jax.ShapeDtypeStruct((heads, latw, tokens), BF16),
            jax.ShapeDtypeStruct((heads * tokens, latw), BF16),
            jax.ShapeDtypeStruct((span, tokens), F32),
        ),
        grid_spec=pltpu.PrefetchScalarGridSpec(
            num_scalar_prefetch=1,
            grid=(heads // pair,),
            in_specs=[
                one(qw, tokens), one(vdim, tokens), one(latw, nope), one(latw, vdim),
                pl.BlockSpec((1, tokens), lambda h, s: (0, 0)),
            ],
            out_specs=[
                one(width, tokens), rows(tokens, width), one(latw, tokens),
                rows(tokens, latw), rows(span // heads, tokens),
            ],
        ),
        compiler_params=pltpu.CompilerParams(vmem_limit_bytes=16 << 20),
        cost_estimate=pl.CostEstimate(
            flops=8 * heads * tokens * latw * nope, transcendentals=0,
            bytes_accessed=16 << 20,
        ),
        name="prepare",
    )(info, qt, gt, w_uk, w_uv, doc_start)


def join(block_ref, core, mine_ref, theirs_ref):
    rows = mine_ref.shape[0]
    block_ref[pl.ds(pl.multiple_of(core * rows, rows), rows)] = mine_ref[...]
    block_ref[pl.ds(pl.multiple_of((1 - core) * rows, rows), rows)] = theirs_ref[...]


def main_kernel(
    info_ref, start_ref, qct_ref, glt_ref, bias_ref, own_ref,
    m3_ref, m2_ref, m1_ref, t3_ref, t2_ref, t1_ref, qc_hbm, gl_hbm,
    ds_ref, keep_ref, send_ref,
    block_s, keys_s, expo_s, dprob_s, p_s, ds_s, qc_s, gl_s, sems, *, factor,
):
    step = pl.program_id(0)
    core = info_ref[0]
    span, tokens = bias_ref.shape
    low = jnp.maximum(start_ref[0] - info_ref[1], 0) // tokens
    pair, latw = glt_ref.shape[:2]
    chunk = 64
    scale = factor * math.log2(math.e)

    @pl.when(step == 0)
    def _():
        pltpu.make_async_copy(qc_hbm, qc_s, sems.at[0]).start()
        pltpu.make_async_copy(gl_hbm, gl_s, sems.at[1]).start()
        for block, (mine, theirs) in enumerate(
            ((m3_ref, t3_ref), (m2_ref, t2_ref), (m1_ref, t1_ref))
        ):
            join(block_s.at[block % 2], core, mine, theirs)
            keys_s[block * tokens : (block + 1) * tokens] = block_s[block % 2].T
        keys_s[BACK * tokens :] = own_ref[...].T

    def fold(x, op):
        return op(x.reshape(-1, 8, tokens), axis=0)

    def heads_from(begin):
        chunks = range(begin, span, chunk)
        for n in range(pair):
            lane = pl.ds(pl.multiple_of((step * pair + n) * tokens, tokens), tokens)
            tops, totals = [], []
            for block in range(begin, span, tokens):
                scores = dot(keys_s[block : block + tokens], qct_ref[n]) * scale
                scores = scores + bias_ref[block : block + tokens]
                for c in range(0, tokens, chunk):
                    s = scores[c : c + chunk]
                    top = jnp.max(fold(s, jnp.max), axis=0, keepdims=True)
                    top = jnp.maximum(top, LOWEST)
                    e = jnp.exp2(s - top)
                    expo_s[n, block + c : block + c + chunk] = e
                    tops.append(top)
                    totals.append(jnp.sum(fold(e, jnp.sum), axis=0, keepdims=True))
            top = functools.reduce(jnp.maximum, tops)
            weights = [jnp.exp2(t - top) for t in tops]
            total = sum(w * t for w, t in zip(weights, totals))
            inverse = 1.0 / total
            delta = jnp.zeros((8, tokens), F32)
            for block in range(begin, span, tokens):
                dprob = dot(keys_s[block : block + tokens, :latw], glt_ref[n])
                for c in range(0, tokens, chunk):
                    at = slice(block + c, block + c + chunk)
                    weight = weights[(block + c - begin) // chunk] * inverse
                    p = (expo_s[n, at] * weight).astype(BF16)
                    dp = dprob[c : c + chunk]
                    p_s[at, lane] = p
                    dprob_s[n, at] = dp
                    delta = delta + fold(p.astype(F32) * dp, jnp.sum)
            delta = jnp.sum(delta, axis=0, keepdims=True)
            for c in chunks:
                at = slice(c, c + chunk)
                ds = (p_s[at, lane].astype(F32) * (dprob_s[n, at] - delta)).astype(BF16)
                ds_s[at, lane] = ds
                ds_ref[n, at] = ds
            if begin:
                zero = jnp.zeros((begin, tokens), BF16)
                ds_ref[n, :begin] = zero

    for block in range(BACK + 1):
        pl.when(low == block)(functools.partial(heads_from, block * tokens))

    @pl.when(step == pl.num_programs(0) - 1)
    def _():
        pltpu.make_async_copy(qc_hbm, qc_s, sems.at[0]).wait()
        pltpu.make_async_copy(gl_hbm, gl_s, sems.at[1]).wait()
        groups, piece = keep_ref.shape[1:3]

        def gradient(block, _):
            at = pl.ds(pl.multiple_of(block * tokens, tokens), tokens)

            def put(column, value):
                sides = value.reshape(groups, CORES, piece, -1)
                zeroth, first = sides[:, 0], sides[:, 1]
                keep_ref[block, :, :, column] = jnp.where(core == 0, zeroth, first).astype(BF16)
                send_ref[block, :, :, column] = jnp.where(core == 0, first, zeroth).astype(BF16)

            key = dot(ds_s[at], qc_s[...]) * factor
            put(slice(0, latw), key[:, :latw] + dot(p_s[at], gl_s[...]))
            put(slice(latw, None), key[:, latw:])
            return 0

        def blank(block, _):
            keep_ref[block] = jnp.zeros(keep_ref.shape[1:], BF16)
            send_ref[block] = jnp.zeros(send_ref.shape[1:], BF16)
            return 0

        lax.fori_loop(0, low, blank, 0)
        lax.fori_loop(low, BACK + 1, gradient, 0)


def attend(info, doc_start, qct, glt, bias, own, mine, theirs, qc, gl, factor, groups, pair=2):
    heads, width, tokens = qct.shape
    latw = glt.shape[1]
    span = bias.shape[0]
    piece = tokens // CORES // groups
    head = lambda d: pl.BlockSpec((pair, d, tokens), lambda h, *_: (h, 0, 0))
    whole = lambda a: pl.BlockSpec(a.shape, lambda h, *_: (0,) * a.ndim)
    out = (BACK + 1, groups, piece, width)
    return pl.pallas_call(
        functools.partial(main_kernel, factor=factor),
        out_shape=(
            pltpu.HBM((heads, span, tokens), BF16),
            jax.ShapeDtypeStruct(out, BF16),
            jax.ShapeDtypeStruct(out, BF16),
        ),
        grid_spec=pltpu.PrefetchScalarGridSpec(
            num_scalar_prefetch=2,
            grid=(heads // pair,),
            in_specs=[head(width), head(latw), whole(bias), whole(own)]
            + [whole(a) for a in (*mine, *theirs)]
            + [pl.BlockSpec(memory_space=pl.ANY)] * 2,
            out_specs=[
                head(span),
                pl.BlockSpec(out, lambda h, *_: (0, 0, 0, 0)),
                pl.BlockSpec(out, lambda h, *_: (0, 0, 0, 0)),
            ],
            scratch_shapes=[
                pltpu.VMEM((2, width, tokens), BF16),
                pltpu.VMEM((span, width), BF16),
                pltpu.VMEM((pair, span, tokens), F32),
                pltpu.VMEM((pair, span, tokens), F32),
                pltpu.VMEM((span, heads * tokens), BF16),
                pltpu.VMEM((span, heads * tokens), BF16),
                pltpu.VMEM(qc.shape, BF16),
                pltpu.VMEM(gl.shape, BF16),
                pltpu.SemaphoreType.DMA((2,)),
            ],
        ),
        compiler_params=pltpu.CompilerParams(vmem_limit_bytes=36 << 20),
        cost_estimate=pl.CostEstimate(
            flops=2 * heads * tokens * span * (2 * width + 2 * latw),
            transcendentals=heads * tokens * span, bytes_accessed=24 << 20,
        ),
        name="attend",
    )(info, doc_start, qct, glt, bias, own, *mine, *theirs, qc, gl)


def query_kernel(
    info_ref, ds_ref, uk_ref, own_ref, m3_ref, m2_ref, m1_ref, t3_ref, t2_ref, t1_ref,
    out_ref, keys_s, *, factor,
):
    core = info_ref[0]
    tokens = own_ref.shape[1]
    pair, latw, nope = uk_ref.shape

    @pl.when(pl.program_id(0) == 0)
    def _():
        for block, (mine, theirs) in enumerate(
            ((m3_ref, t3_ref), (m2_ref, t2_ref), (m1_ref, t1_ref))
        ):
            join(keys_s.at[:, pl.ds(block * tokens, tokens)], core, mine, theirs)
        keys_s[:, BACK * tokens :] = own_ref[...]

    for n in range(pair):
        dq = dot(keys_s[...], ds_ref[n]) * factor
        dq_nope = dot(uk_ref[n], dq[:latw].astype(BF16), ((0,), (0,)))
        out_ref[n, :nope] = dq_nope.astype(BF16)
        out_ref[n, nope:] = dq[latw:].astype(BF16)


def query_gradient(info, ds, w_uk, own, mine, theirs, factor, pair=2):
    heads, span, tokens = ds.shape
    latw, nope = w_uk.shape[1:]
    width = own.shape[0]
    qw = nope + width - latw
    whole = lambda a: pl.BlockSpec(a.shape, lambda h, s: (0,) * a.ndim)
    return pl.pallas_call(
        functools.partial(query_kernel, factor=factor),
        out_shape=jax.ShapeDtypeStruct((heads, qw, tokens), BF16),
        grid_spec=pltpu.PrefetchScalarGridSpec(
            num_scalar_prefetch=1,
            grid=(heads // pair,),
            in_specs=[
                pl.BlockSpec((pair, span, tokens), lambda h, s: (h, 0, 0)),
                pl.BlockSpec((pair, latw, nope), lambda h, s: (h, 0, 0)),
                whole(own),
            ]
            + [whole(a) for a in (*mine, *theirs)],
            out_specs=pl.BlockSpec((pair, qw, tokens), lambda h, s: (h, 0, 0)),
            scratch_shapes=[pltpu.VMEM((width, span), BF16)],
        ),
        compiler_params=pltpu.CompilerParams(vmem_limit_bytes=16 << 20),
        cost_estimate=pl.CostEstimate(
            flops=2 * heads * tokens * (span * width + latw * nope),
            transcendentals=0, bytes_accessed=8 << 20,
        ),
        name="query_gradient",
    )(info, ds, w_uk, own, *mine, *theirs)


def along_seq(distance, crossings=True):
    devices = lax.axis_size("seq")
    pairs = []
    for source in range(devices):
        target = source + distance
        if 0 <= target < devices:
            crossing = (2 * source < devices) != (2 * target < devices)
            if crossings or not crossing:
                pairs += between(source, target, crossing)
    return pairs


def between(source, target, mirrored=False):
    heads = lax.axis_size("head")
    pairs = []
    for head in range(heads):
        chip, core = divmod(head, CORES)
        if mirrored:
            chip = heads // CORES - 1 - chip
        pairs.append((source * heads + head, target * heads + chip * CORES + core))
    return pairs


def send(value, pairs):
    return lax.ppermute(value, ("seq", "head"), pairs)


def in_hbm(value):
    return pltpu.with_memory_space_constraint(value, pltpu.HBM)


def swap_cores(value):
    return lax.ppermute(value, "head", [(k, k ^ 1) for k in range(lax.axis_size("head"))])


def shards(queries, grad_out, latent, w_uk, w_uv, doc_start):
    tokens, width = latent.shape
    factor = queries.shape[2] ** (-0.5)
    seq, head = lax.axis_index("seq"), lax.axis_index("head")
    heads = lax.axis_size("head")
    chips = heads // CORES
    core, chip = head % CORES, head // CORES
    half = width // CORES

    own = latent.T
    part = lax.dynamic_slice_in_dim(own, core * half, half, 0)
    far = send(part, along_seq(3))
    near = [send(part, along_seq(distance, False)) for distance in (2, 1)]

    middle = lax.axis_size("seq") // 2
    after, next_one, next_two = middle, middle + 1, middle + 2
    relays = (between(next_one, after) + between(next_two, next_one), between(next_two, after))
    returns = (between(after, next_one) + between(next_one, next_two), between(after, next_two))

    info = jnp.stack([core, (seq - BACK) * tokens]).astype(jnp.int32)
    qt = jnp.transpose(queries, (1, 2, 0))
    gt = jnp.transpose(grad_out, (1, 2, 0))
    far, gt = lax.optimization_barrier((far, gt))
    relayed = [send(far, relay) for relay in relays]
    prepared = prepare(
        info, in_hbm(qt), gt, in_hbm(w_uk), in_hbm(w_uv), in_hbm(doc_start[None])
    )
    near, relayed, prepared = lax.optimization_barrier((near[::-1], relayed, prepared))
    qct, qc, glt, gl, bias = prepared
    mine = [far] + [direct + other for direct, other in zip(near[::-1], relayed)]
    theirs = [swap_cores(piece) for piece in mine]

    ds, keep, away = attend(
        info, doc_start, qct, glt, bias, own, mine, theirs, qc, gl, factor, chips
    )
    arrived = swap_cores(away)
    far, *near, total = list(keep + arrived)
    for piece, route in zip(near, returns):
        far = far + send(piece, route)
    far, near = lax.optimization_barrier((far, near))
    back = [send(piece, along_seq(-distance, False)) for piece, distance in zip(near, (2, 1))]
    back.append(send(far, along_seq(-3)))
    dq = query_gradient(info, in_hbm(ds), in_hbm(w_uk), own, mine, theirs, factor)
    back, dq = lax.optimization_barrier((back[::-1], dq))
    total = total.astype(F32)
    for piece in back:
        total = total + piece.astype(F32)
    grad_query = jnp.transpose(dq, (2, 0, 1))
    return grad_query, scatter_sum(total, chip)


def scatter_sum(total, chip):
    chips, rows, width = total.shape
    bit = 1
    while bit < chips:
        mine = chip // bit % 2
        halves = total.reshape(-1, 2, rows, width)
        away = lax.dynamic_index_in_dim(halves, 1 - mine, 1, False).astype(BF16)
        route = [(k, k ^ (bit * CORES)) for k in range(chips * CORES)]
        arrived = lax.ppermute(away, "head", route)
        total = lax.dynamic_index_in_dim(halves, mine, 1, False) + arrived.astype(F32)
        bit *= 2
    return total[0]


def solution(mesh):
    placed = (
        P("seq", "head", None),
        P("seq", "head", None),
        P("seq", None),
        P("head", None, None),
        P("head", None, None),
        P("seq"),
    )
    return jax.shard_map(
        shards,
        mesh=mesh,
        in_specs=placed,
        out_specs=(P("seq", "head", None), P(("seq", "head"), None)),
        check_vma=False,
    )
```

profile of v0, /device:TPU:132, one launch (start us, length us, event | category | flops | bytes accessed | tf_op | source)
XLA Modules:
  0.0 86.1 jit_solution(6067886061620274549)
XLA Ops:
  0.6 0.9 %dynamic-slice_bitcast_fusion = bf16[288,256]{1,0:T(8,128)(2,1)S(1)} fusion(bf16[256,576]{0,1:T(8,128)(2,1)} %param.8, s32[]{:T(128)S(6)} %select_n.41), kind=kLoop, calls=%fused_computation.11 | loop fusion | bytes 294916 | tf_op jit(solution)/shard_map/dynamic_slice | solution.py:337
  1.6 4.9 %collective-permute-start.2 = (bf16[288,256]{1,0:T(8,128)(2,1)S(1)}, bf16[288,256]{1,0:T(8,128)(2,1)S(1)}, u32[]{:S(2)}, u32[]{:S(2)}) collective-permute-start(bf16[288,256]{1,0:T(8,128)(2,1)S(1)} %dynamic-slice_bitcast_fusion), channel_id=1, source_target_pairs={{0,24},{1,25},{2,26},{3,27},{4,28},{5,29},{6,30},{7,31},{8,32},{9,... | collective-permute-start | bytes 442376 | tf_op jit(solution)/shard_map/ppermute | solution.py:316
  6.5 3.2 %collective-permute-start.1 = (bf16[288,256]{1,0:T(8,128)(2,1)S(1)}, bf16[288,256]{1,0:T(8,128)(2,1)S(1)}, u32[]{:S(2)}, u32[]{:S(2)}) collective-permute-start(bf16[288,256]{1,0:T(8,128)(2,1)S(1)} %dynamic-slice_bitcast_fusion), channel_id=1, source_target_pairs={{0,16},{1,17},{2,18},{3,19},{4,20},{5,21},{6,22},{7,23},{8,24},{9,... | collective-permute-start | bytes 442376 | tf_op jit(solution)/shard_map/ppermute | solution.py:316
  9.7 2.9 %collective-permute-start = (bf16[288,256]{1,0:T(8,128)(2,1)S(1)}, bf16[288,256]{1,0:T(8,128)(2,1)S(1)}, u32[]{:S(2)}, u32[]{:S(2)}) collective-permute-start(bf16[288,256]{1,0:T(8,128)(2,1)S(1)} %dynamic-slice_bitcast_fusion), channel_id=1, source_target_pairs={{0,8},{1,9},{2,10},{3,11},{4,12},{5,13},{6,14},{7,15},{8,16},{9,17... | collective-permute-start | bytes 442376 | tf_op jit(solution)/shard_map/ppermute | solution.py:316
  12.6 1.3 %copy.8 = bf16[256,8,128]{0,2,1:T(8,128)(2,1)S(1)} copy(bf16[256,8,128]{2,1,0:T(8,128)(2,1)} %param.7) | data formatting | bytes 1048576 | tf_op args[1]
  13.9 0.0 collective-permute-done.2.m3_ref
  13.9 0.7 collective-permute-start.4
  14.6 0.7 collective-permute-start.3
  15.3 0.1 pad_add_fusion.info_ref
  15.4 0.0 collective-permute-start.5
  15.4 0.0 copy-start
  15.4 0.0 copy-start.1
  15.4 5.0 %prepare.1 = (bf16[8,576,256]{2,1,0:T(8,128)(2,1)S(1)}, bf16[2048,576]{1,0:T(8,128)(2,1)S(1)}, bf16[8,512,256]{2,1,0:T(8,128)(2,1)S(1)}, bf16[2048,512]{1,0:T(8,128)(2,1)S(1)}, f32[1024,256]{1,0:T(8,128)S(1)}) custom-call(s32[2]{0:T(128)S(1)} %pad_add_fusion.info_ref, bf16[8,192,256]{2,1,0:T(8,128)(2,1)} %bitcast.41, bf16[8,128,256]{2,1,0:T(8,128)(2,1)S(1)} %bitcast.35, ...), custom_call_target="tpu_custom_call" | custom-call | flops 1073741824 | bytes 16777216 | tf_op jit(solution)/shard_map/prepare/pallas_call | solution.py:55
  20.5 0.0 collective-permute-done.1
  20.5 0.0 collective-permute-done
  20.5 0.0 collective-permute-done.4
  20.5 0.0 collective-permute-done.3
  20.6 0.6 collective-permute-start.7
  21.2 0.1 collective-permute-start.6
  21.3 0.0 collective-permute-done.5.t3_ref
  21.3 0.8 collective-permute-done.7.t1_ref
  22.1 0.5 collective-permute-done.6.t2_ref
  22.6 0.0 copy-done
  22.6 0.0 copy-done.1
  22.6 14.1 %attend.1 = (bf16[8,1024,256]{2,1,0:T(8,128)(2,1)}, bf16[4,4,32,576]{3,2,1,0:T(8,128)(2,1)S(1)}, bf16[4,4,32,576]{3,2,1,0:T(8,128)(2,1)S(1)}) custom-call(s32[2]{0:T(128)S(1)} %pad_add_fusion.info_ref, s32[256]{0:T(256)S(1)} %copy-done.1, bf16[8,576,256]{2,1,0:T(8,128)(2,1)S(1)} %get-tuple-element.35.qct_ref, ...), custom_call_target="tpu_custom_call" | custom-call | flops 9126805504 | bytes 25165824 | tf_op jit(solution)/shard_map/attend/pallas_call | solution.py:200
  36.7 0.2 collective-permute-start.8
  36.9 2.0 %collective-permute-done.8 = bf16[4,4,32,576]{3,2,1,0:T(8,128)(2,1)S(1)} collective-permute-done((bf16[4,4,32,576]{3,2,1,0:T(8,128)(2,1)S(1)}, bf16[4,4,32,576]{3,2,1,0:T(8,128)(2,1)S(1)}, u32[]{:S(2)}, u32[]{:S(2)}) %collective-permute-start.8) | collective-permute-done | bytes 589856 | tf_op jit(solution)/shard_map/ppermute | solution.py:324
  38.9 0.2 add.67
  39.1 0.7 collective-permute-start.9
  39.8 0.7 collective-permute-start.10
  40.5 0.0 collective-permute-done.9
  40.5 0.0 collective-permute-done.10
  40.6 4.1 %collective-permute-start.11 = (bf16[4,32,576]{2,1,0:T(8,128)(2,1)S(1)}, bf16[4,32,576]{2,1,0:T(8,128)(2,1)S(1)}, u32[]{:S(2)}, u32[]{:S(2)}) collective-permute-start(bf16[4,32,576]{2,1,0:T(8,128)(2,1)S(1)} %fusion.3), channel_id=1, source_target_pairs={{24,0},{25,1},{26,2},{27,3},{28,4},{29,5},{30,6},{31,7},{32,8},{33... | collective-permute-start | bytes 442376 | tf_op jit(solution)/shard_map/ppermute | solution.py:316
  44.6 1.9 %collective-permute-start.12 = (bf16[4,32,576]{2,1,0:T(8,128)(2,1)S(1)}, bf16[4,32,576]{2,1,0:T(8,128)(2,1)S(1)}, u32[]{:S(2)}, u32[]{:S(2)}) collective-permute-start(bf16[4,32,576]{2,1,0:T(8,128)(2,1)S(1)} %get-tuple-element.47), channel_id=1, source_target_pairs={{8,0},{9,1},{10,2},{11,3},{12,4},{13,5},{14,6},{15,7},{16,8},{17,9... | collective-permute-start | bytes 442376 | tf_op jit(solution)/shard_map/ppermute | solution.py:316
  46.6 19.8 %collective-permute-start.13 = (bf16[4,32,576]{2,1,0:T(8,128)(2,1)S(1)}, bf16[4,32,576]{2,1,0:T(8,128)(2,1)S(1)}, u32[]{:S(2)}, u32[]{:S(2)}) collective-permute-start(bf16[4,32,576]{2,1,0:T(8,128)(2,1)S(1)} %get-tuple-element.48), channel_id=1, source_target_pairs={{16,0},{17,1},{18,2},{19,3},{20,4},{21,5},{22,6},{23,7},{24,8},{25... | collective-permute-start | bytes 442376 | tf_op jit(solution)/shard_map/ppermute | solution.py:316
  66.4 9.3 %query_gradient.1 = bf16[8,192,256]{2,1,0:T(8,128)(2,1)} custom-call(s32[2]{0:T(128)S(1)} %pad_add_fusion.info_ref, bf16[8,1024,256]{2,1,0:T(8,128)(2,1)} %get-tuple-element.49.ds_ref, bf16[8,512,128]{2,1,0:T(8,128)(2,1)} %uk_ref.3, bf16[576,256]{1,0:T(8,128)(2,1)S(1)} %bitcast.37, bf16[288,256]{1,0:T(8,128)(2,1)S(1)} %collective-permute-done.2.m3_ref, ...), custom_call_target="tpu_custom_call" | custom-call | flops 2684354560 | bytes 8388608 | tf_op jit(solution)/shard_map/query_gradient/pallas_call | solution.py:268
  75.7 0.0 collective-permute-done.11
  75.7 0.0 collective-permute-done.12
  75.7 0.0 collective-permute-done.13
  75.7 0.1 fusion.1
  75.9 0.1 collective-permute-start.14
  76.0 4.4 %collective-permute-done.14 = bf16[2,32,576]{2,1,0:T(8,128)(2,1)S(1)} collective-permute-done((bf16[2,32,576]{2,1,0:T(8,128)(2,1)S(1)}, bf16[2,32,576]{2,1,0:T(8,128)(2,1)S(1)}, u32[]{:S(2)}, u32[]{:S(2)}) %collective-permute-start.14) | collective-permute-done | bytes 73760 | tf_op jit(solution)/shard_map/ppermute | solution.py:386
  80.4 0.6 collective-permute-start.15
  81.0 4.4 %collective-permute-done.15 = bf16[1,32,576]{2,1,0:T(8,128)(2,1)S(1)} collective-permute-done((bf16[1,32,576]{2,1,0:T(8,128)(2,1)S(1)}, bf16[1,32,576]{2,1,0:T(8,128)(2,1)S(1)}, u32[]{:S(2)}, u32[]{:S(2)}) %collective-permute-start.15) | collective-permute-done | bytes 36896 | tf_op jit(solution)/shard_map/ppermute | solution.py:386
  85.4 0.6 add_bitcast_fusion
  (7 shorter events, 0.2 us)
Async XLA Ops:
  1.6 12.3 %collective-permute-start.2 = (bf16[288,256]{1,0:T(8,128)(2,1)S(1)}, bf16[288,256]{1,0:T(8,128)(2,1)S(1)}, u32[]{:S(2)}, u32[]{:S(2)}) collective-permute-start(bf16[288,256]{1,0:T(8,128)(2,1)S(1)} %dynamic-slice_bitcast_fusion), channel_id=1, source_target_pairs={{0,24},{1,25},{2,26},{3,27},{4,28},{5,29},{6,30},{7,31},{8,32},{9,... | collective-permute-start | bytes 442376 | tf_op jit(solution)/shard_map/ppermute | solution.py:316
  6.5 14.0 %collective-permute-start.1 = (bf16[288,256]{1,0:T(8,128)(2,1)S(1)}, bf16[288,256]{1,0:T(8,128)(2,1)S(1)}, u32[]{:S(2)}, u32[]{:S(2)}) collective-permute-start(bf16[288,256]{1,0:T(8,128)(2,1)S(1)} %dynamic-slice_bitcast_fusion), channel_id=1, source_target_pairs={{0,16},{1,17},{2,18},{3,19},{4,20},{5,21},{6,22},{7,23},{8,24},{9,... | collective-permute-start | bytes 442376 | tf_op jit(solution)/shard_map/ppermute | solution.py:316
  9.7 10.8 %collective-permute-start = (bf16[288,256]{1,0:T(8,128)(2,1)S(1)}, bf16[288,256]{1,0:T(8,128)(2,1)S(1)}, u32[]{:S(2)}, u32[]{:S(2)}) collective-permute-start(bf16[288,256]{1,0:T(8,128)(2,1)S(1)} %dynamic-slice_bitcast_fusion), channel_id=1, source_target_pairs={{0,8},{1,9},{2,10},{3,11},{4,12},{5,13},{6,14},{7,15},{8,16},{9,17... | collective-permute-start | bytes 442376 | tf_op jit(solution)/shard_map/ppermute | solution.py:316
  13.9 6.6 %collective-permute-start.4 = (bf16[288,256]{1,0:T(8,128)(2,1)S(1)}, bf16[288,256]{1,0:T(8,128)(2,1)S(1)}, u32[]{:S(2)}, u32[]{:S(2)}) collective-permute-start(bf16[288,256]{1,0:T(8,128)(2,1)S(1)} %collective-permute-done.2.m3_ref), channel_id=1, source_target_pairs={{144,128},{145,129},{146,130},{147,131},{148,132},{149,133},{150,1... | collective-permute-start | bytes 442376 | tf_op jit(solution)/shard_map/ppermute | solution.py:316
  14.6 5.9 %collective-permute-start.3 = (bf16[288,256]{1,0:T(8,128)(2,1)S(1)}, bf16[288,256]{1,0:T(8,128)(2,1)S(1)}, u32[]{:S(2)}, u32[]{:S(2)}) collective-permute-start(bf16[288,256]{1,0:T(8,128)(2,1)S(1)} %collective-permute-done.2.m3_ref), channel_id=1, source_target_pairs={{136,128},{137,129},{138,130},{139,131},{140,132},{141,133},{142,1... | collective-permute-start | bytes 442376 | tf_op jit(solution)/shard_map/ppermute | solution.py:316
  15.4 5.9 %collective-permute-start.5 = (bf16[288,256]{1,0:T(8,128)(2,1)S(1)}, bf16[288,256]{1,0:T(8,128)(2,1)S(1)}, u32[]{:S(2)}, u32[]{:S(2)}) collective-permute-start(bf16[288,256]{1,0:T(8,128)(2,1)S(1)} %collective-permute-done.2.m3_ref), channel_id=1, source_target_pairs={{0,1},{1,0},{2,3},{3,2},{4,5},{5,4},{6,7},{7,6},{8,9},{9,8},{10,11... | collective-permute-start | bytes 442376 | tf_op jit(solution)/shard_map/ppermute | solution.py:324
  15.4 7.2 %copy-start = (bf16[256,576]{0,1:T(8,128)(2,1)S(1)}, bf16[256,576]{0,1:T(8,128)(2,1)}, u32[]{:S(2)}) copy-start(bf16[256,576]{0,1:T(8,128)(2,1)} %param.8) | copy-start | bytes 884740
  15.4 7.2 %copy-start.1 = (s32[256]{0:T(256)S(1)}, s32[256]{0:T(256)}, u32[]{:S(2)}) copy-start(s32[256]{0:T(256)} %start_ref.1) | copy-start | bytes 3076
  20.6 1.6 %collective-permute-start.7 = (bf16[288,256]{1,0:T(8,128)(2,1)S(1)}, bf16[288,256]{1,0:T(8,128)(2,1)S(1)}, u32[]{:S(2)}, u32[]{:S(2)}) collective-permute-start(bf16[288,256]{1,0:T(8,128)(2,1)S(1)} %add.66.m1_ref), channel_id=1, source_target_pairs={{0,1},{1,0},{2,3},{3,2},{4,5},{5,4},{6,7},{7,6},{8,9},{9,8},{10,11... | collective-permute-start | bytes 442376 | tf_op jit(solution)/shard_map/ppermute | solution.py:324
  21.2 1.5 %collective-permute-start.6 = (bf16[288,256]{1,0:T(8,128)(2,1)S(1)}, bf16[288,256]{1,0:T(8,128)(2,1)S(1)}, u32[]{:S(2)}, u32[]{:S(2)}) collective-permute-start(bf16[288,256]{1,0:T(8,128)(2,1)S(1)} %add.65.m2_ref), channel_id=1, source_target_pairs={{0,1},{1,0},{2,3},{3,2},{4,5},{5,4},{6,7},{7,6},{8,9},{9,8},{10,11... | collective-permute-start | bytes 442376 | tf_op jit(solution)/shard_map/ppermute | solution.py:324
  36.7 2.2 %collective-permute-start.8 = (bf16[4,4,32,576]{3,2,1,0:T(8,128)(2,1)S(1)}, bf16[4,4,32,576]{3,2,1,0:T(8,128)(2,1)S(1)}, u32[]{:S(2)}, u32[]{:S(2)}) collective-permute-start(bf16[4,4,32,576]{3,2,1,0:T(8,128)(2,1)S(1)} %get-tuple-element.45), channel_id=1, source_target_pairs={{0,1},{1,0},{2,3},{3,2},{4,5},{5,4},{6,7},{7,6},{8,9},{9,8},{10,11... | collective-permute-start | bytes 1769480 | tf_op jit(solution)/shard_map/ppermute | solution.py:324
  39.1 1.4 %collective-permute-start.9 = (bf16[4,32,576]{2,1,0:T(8,128)(2,1)S(1)}, bf16[4,32,576]{2,1,0:T(8,128)(2,1)S(1)}, u32[]{:S(2)}, u32[]{:S(2)}) collective-permute-start(bf16[4,32,576]{2,1,0:T(8,128)(2,1)S(1)} %get-tuple-element.48), channel_id=1, source_target_pairs={{128,136},{129,137},{130,138},{131,139},{132,140},{133,141},{134,1... | collective-permute-start | bytes 442376 | tf_op jit(solution)/shard_map/ppermute | solution.py:316
  39.8 0.7 collective-permute-start.10
  40.6 35.2 %collective-permute-start.11 = (bf16[4,32,576]{2,1,0:T(8,128)(2,1)S(1)}, bf16[4,32,576]{2,1,0:T(8,128)(2,1)S(1)}, u32[]{:S(2)}, u32[]{:S(2)}) collective-permute-start(bf16[4,32,576]{2,1,0:T(8,128)(2,1)S(1)} %fusion.3), channel_id=1, source_target_pairs={{24,0},{25,1},{26,2},{27,3},{28,4},{29,5},{30,6},{31,7},{32,8},{33... | collective-permute-start | bytes 442376 | tf_op jit(solution)/shard_map/ppermute | solution.py:316
  44.6 31.1 %collective-permute-start.12 = (bf16[4,32,576]{2,1,0:T(8,128)(2,1)S(1)}, bf16[4,32,576]{2,1,0:T(8,128)(2,1)S(1)}, u32[]{:S(2)}, u32[]{:S(2)}) collective-permute-start(bf16[4,32,576]{2,1,0:T(8,128)(2,1)S(1)} %get-tuple-element.47), channel_id=1, source_target_pairs={{8,0},{9,1},{10,2},{11,3},{12,4},{13,5},{14,6},{15,7},{16,8},{17,9... | collective-permute-start | bytes 442376 | tf_op jit(solution)/shard_map/ppermute | solution.py:316
  46.6 29.2 %collective-permute-start.13 = (bf16[4,32,576]{2,1,0:T(8,128)(2,1)S(1)}, bf16[4,32,576]{2,1,0:T(8,128)(2,1)S(1)}, u32[]{:S(2)}, u32[]{:S(2)}) collective-permute-start(bf16[4,32,576]{2,1,0:T(8,128)(2,1)S(1)} %get-tuple-element.48), channel_id=1, source_target_pairs={{16,0},{17,1},{18,2},{19,3},{20,4},{21,5},{22,6},{23,7},{24,8},{25... | collective-permute-start | bytes 442376 | tf_op jit(solution)/shard_map/ppermute | solution.py:316
  75.9 4.5 %collective-permute-start.14 = (bf16[2,32,576]{2,1,0:T(8,128)(2,1)S(1)}, bf16[2,32,576]{2,1,0:T(8,128)(2,1)S(1)}, u32[]{:S(2)}, u32[]{:S(2)}) collective-permute-start(bf16[2,32,576]{2,1,0:T(8,128)(2,1)S(1)} %fusion.4), channel_id=1, source_target_pairs={{0,2},{1,3},{2,0},{3,1},{4,6},{5,7},{6,4},{7,5},{8,10},{9,11},{10,... | collective-permute-start | bytes 221192 | tf_op jit(solution)/shard_map/ppermute | solution.py:386
  80.4 5.0 %collective-permute-start.15 = (bf16[1,32,576]{2,1,0:T(8,128)(2,1)S(1)}, bf16[1,32,576]{2,1,0:T(8,128)(2,1)S(1)}, u32[]{:S(2)}, u32[]{:S(2)}) collective-permute-start(bf16[1,32,576]{2,1,0:T(8,128)(2,1)S(1)} %dynamic-slice_convert_fusion), channel_id=1, source_target_pairs={{0,4},{1,5},{2,6},{3,7},{4,0},{5,1},{6,2},{7,3},{8,12},{9,13},{10,... | collective-permute-start | bytes 110600 | tf_op jit(solution)/shard_map/ppermute | solution.py:386
where the time goes:
time: 87.1 us; the launch traced here: 86.1 us
  starting transfers between devices  41.1 us (47%)
  Pallas kernels  28.4 us (33%)
  waiting for transfers between devices  12.1 us (14%)
  local copies, waits for them, and re-layouts  2.32 us (3%)
  other arithmetic  1.09 us (1%)
  between operations  1.01 us (1%)
    ppermute x10, starting transfers between devices, send(): return lax.ppermute(value, ('seq', 'head'), pairs)  39.5 us
    pallas_call x1, Pallas kernels, attend(): pl.pallas_call(functools.partial(main_kernel, factor=factor), out_shape=(...  14.1 us
    pallas_call x1, Pallas kernels, query_gradient(): pl.pallas_call(functools.partial(query_kernel, factor=factor), out_shape=...  9.31 us
    ppermute x2, waiting for transfers between devices, scatter_sum(): arrived = lax.ppermute(away, 'head', route)  8.81 us
    pallas_call x1, Pallas kernels, prepare(): pl.pallas_call(prepare_kernel, out_shape=(jax.ShapeDtypeStruct((heads, wi...  5.04 us
    ppermute x4, waiting for transfers between devices, swap_cores(): lax.ppermute(value, 'head', [(k, k ^ 1) for k in range(lax.axis_size('hea...  3.28 us
  transfers between devices with their start and end apart: 16, of which 5 were waited for; matrix products, arithmetic and copies ran while one was open for 2% of the time, Pallas kernels for 17%

commit v1 on v0

--- a/solution.py
+++ b/solution.py
@@ -19,6 +19,8 @@
 
 
 LOWEST = -1e30
+CHUNK = 64
+PAIR = 2
 
 
 def prepare_kernel(
@@ -30,11 +32,11 @@
     for n in range(pair):
         uk, uv = uk_ref[n], uv_ref[n]
         rows = slice(n * tokens, (n + 1) * tokens)
-        qct_ref[n, :latw] = dot(uk, qt_ref[n, :nope]).astype(BF16)
-        qct_ref[n, latw:] = qt_ref[n, nope:]
+        qct_ref[:latw, rows] = dot(uk, qt_ref[n, :nope]).astype(BF16)
+        qct_ref[latw:, rows] = qt_ref[n, nope:]
         qc_ref[rows, :latw] = dot(qt_ref[n, :nope].T, uk, ((1,), (1,))).astype(BF16)
         qc_ref[rows, latw:] = qt_ref[n, nope:].T
-        glt_ref[n] = dot(uv, gt_ref[n]).astype(BF16)
+        glt_ref[:, rows] = dot(uv, gt_ref[n]).astype(BF16)
         gl_ref[rows] = dot(gt_ref[n].T, uv, ((1,), (1,))).astype(BF16)
     shape = bias_ref.shape
     row = pl.program_id(0) * shape[0] + lax.broadcasted_iota(jnp.int32, shape, 0)
@@ -52,12 +54,13 @@
     span = (BACK + 1) * tokens
     one = lambda *dims: pl.BlockSpec((pair, *dims), lambda h, s: (h, 0, 0))
     rows = lambda n, d: pl.BlockSpec((pair * n, d), lambda h, s: (h, 0))
+    lanes = lambda d, n: pl.BlockSpec((d, pair * n), lambda h, s: (0, h))
     return pl.pallas_call(
         prepare_kernel,
         out_shape=(
-            jax.ShapeDtypeStruct((heads, width, tokens), BF16),
+            jax.ShapeDtypeStruct((width, heads * tokens), BF16),
             jax.ShapeDtypeStruct((heads * tokens, width), BF16),
-            jax.ShapeDtypeStruct((heads, latw, tokens), BF16),
+            jax.ShapeDtypeStruct((latw, heads * tokens), BF16),
             jax.ShapeDtypeStruct((heads * tokens, latw), BF16),
             jax.ShapeDtypeStruct((span, tokens), F32),
         ),
@@ -69,7 +72,7 @@
                 pl.BlockSpec((1, tokens), lambda h, s: (0, 0)),
             ],
             out_specs=[
-                one(width, tokens), rows(tokens, width), one(latw, tokens),
+                lanes(width, tokens), rows(tokens, width), lanes(latw, tokens),
                 rows(tokens, latw), rows(span // heads, tokens),
             ],
         ),
@@ -98,8 +101,8 @@
     core = info_ref[0]
     span, tokens = bias_ref.shape
     low = jnp.maximum(start_ref[0] - info_ref[1], 0) // tokens
-    pair, latw = glt_ref.shape[:2]
-    chunk = 64
+    latw, lanes = glt_ref.shape
+    chunk = CHUNK * tokens // lanes
     scale = factor * math.log2(math.e)
 
     @pl.when(step == 0)
@@ -114,48 +117,45 @@
         keys_s[BACK * tokens :] = own_ref[...].T
 
     def fold(x, op):
-        return op(x.reshape(-1, 8, tokens), axis=0)
+        return op(x.reshape(-1, 8, lanes), axis=0)
 
     def heads_from(begin):
-        chunks = range(begin, span, chunk)
-        for n in range(pair):
-            lane = pl.ds(pl.multiple_of((step * pair + n) * tokens, tokens), tokens)
-            tops, totals = [], []
-            for block in range(begin, span, tokens):
-                scores = dot(keys_s[block : block + tokens], qct_ref[n]) * scale
-                scores = scores + bias_ref[block : block + tokens]
-                for c in range(0, tokens, chunk):
-                    s = scores[c : c + chunk]
-                    top = jnp.max(fold(s, jnp.max), axis=0, keepdims=True)
-                    top = jnp.maximum(top, LOWEST)
-                    e = jnp.exp2(s - top)
-                    expo_s[n, block + c : block + c + chunk] = e
-                    tops.append(top)
-                    totals.append(jnp.sum(fold(e, jnp.sum), axis=0, keepdims=True))
-            top = functools.reduce(jnp.maximum, tops)
-            weights = [jnp.exp2(t - top) for t in tops]
-            total = sum(w * t for w, t in zip(weights, totals))
-            inverse = 1.0 / total
-            delta = jnp.zeros((8, tokens), F32)
-            for block in range(begin, span, tokens):
-                dprob = dot(keys_s[block : block + tokens, :latw], glt_ref[n])
-                for c in range(0, tokens, chunk):
-                    at = slice(block + c, block + c + chunk)
-                    weight = weights[(block + c - begin) // chunk] * inverse
-                    p = (expo_s[n, at] * weight).astype(BF16)
-                    dp = dprob[c : c + chunk]
-                    p_s[at, lane] = p
-                    dprob_s[n, at] = dp
-                    delta = delta + fold(p.astype(F32) * dp, jnp.sum)
-            delta = jnp.sum(delta, axis=0, keepdims=True)
-            for c in chunks:
-                at = slice(c, c + chunk)
-                ds = (p_s[at, lane].astype(F32) * (dprob_s[n, at] - delta)).astype(BF16)
-                ds_s[at, lane] = ds
-                ds_ref[n, at] = ds
-            if begin:
-                zero = jnp.zeros((begin, tokens), BF16)
-                ds_ref[n, :begin] = zero
+        lane = pl.ds(pl.multiple_of(step * lanes, lanes), lanes)
+        tops, totals = [], []
+        for block in range(begin, span, tokens):
+            scores = dot(keys_s[block : block + tokens], qct_ref[...])
+            for c in range(0, tokens, chunk):
+                at = slice(block + c, block + c + chunk)
+                bias = jnp.concatenate([bias_ref[at]] * (lanes // tokens), 1)
+                s = scores[c : c + chunk] * scale + bias
+                top = jnp.max(fold(s, jnp.max), axis=0, keepdims=True)
+                top = jnp.maximum(top, LOWEST)
+                e = jnp.exp2(s - top)
+                expo_s[at] = e
+                tops.append(top)
+                totals.append(jnp.sum(fold(e, jnp.sum), axis=0, keepdims=True))
+        top = functools.reduce(jnp.maximum, tops)
+        weights = [jnp.exp2(t - top) for t in tops]
+        inverse = 1.0 / sum(w * t for w, t in zip(weights, totals))
+        delta = jnp.zeros((8, lanes), F32)
+        for block in range(begin, span, tokens):
+            dprob = dot(keys_s[block : block + tokens, :latw], glt_ref[...])
+            for c in range(0, tokens, chunk):
+                at = slice(block + c, block + c + chunk)
+                weight = weights[(block + c - begin) // chunk] * inverse
+                p = (expo_s[at] * weight).astype(BF16)
+                dp = dprob[c : c + chunk]
+                p_s[at, lane] = p
+                dprob_s[at] = dp
+                delta = delta + fold(p.astype(F32) * dp, jnp.sum)
+        delta = jnp.sum(delta, axis=0, keepdims=True)
+        for c in range(begin, span, chunk):
+            at = slice(c, c + chunk)
+            ds = (p_s[at, lane].astype(F32) * (dprob_s[at] - delta)).astype(BF16)
+            ds_s[at, lane] = ds
+            ds_ref[at] = ds
+        if begin:
+            ds_ref[:begin] = jnp.zeros((begin, lanes), BF16)
 
     for block in range(BACK + 1):
         pl.when(low == block)(functools.partial(heads_from, block * tokens))
@@ -189,24 +189,25 @@
         lax.fori_loop(low, BACK + 1, gradient, 0)
 
 
-def attend(info, doc_start, qct, glt, bias, own, mine, theirs, qc, gl, factor, groups, pair=2):
-    heads, width, tokens = qct.shape
-    latw = glt.shape[1]
-    span = bias.shape[0]
+def attend(info, doc_start, qct, glt, bias, own, mine, theirs, qc, gl, factor, groups, pair=PAIR):
+    width, queries = qct.shape
+    latw = glt.shape[0]
+    span, tokens = bias.shape
+    lanes = pair * tokens
     piece = tokens // CORES // groups
-    head = lambda d: pl.BlockSpec((pair, d, tokens), lambda h, *_: (h, 0, 0))
+    head = lambda d: pl.BlockSpec((d, lanes), lambda h, *_: (0, h))
     whole = lambda a: pl.BlockSpec(a.shape, lambda h, *_: (0,) * a.ndim)
     out = (BACK + 1, groups, piece, width)
     return pl.pallas_call(
         functools.partial(main_kernel, factor=factor),
         out_shape=(
-            pltpu.HBM((heads, span, tokens), BF16),
+            pltpu.HBM((span, queries), BF16),
             jax.ShapeDtypeStruct(out, BF16),
             jax.ShapeDtypeStruct(out, BF16),
         ),
         grid_spec=pltpu.PrefetchScalarGridSpec(
             num_scalar_prefetch=2,
-            grid=(heads // pair,),
+            grid=(queries // lanes,),
             in_specs=[head(width), head(latw), whole(bias), whole(own)]
             + [whole(a) for a in (*mine, *theirs)]
             + [pl.BlockSpec(memory_space=pl.ANY)] * 2,
@@ -218,19 +219,19 @@
             scratch_shapes=[
                 pltpu.VMEM((2, width, tokens), BF16),
                 pltpu.VMEM((span, width), BF16),
-                pltpu.VMEM((pair, span, tokens), F32),
-                pltpu.VMEM((pair, span, tokens), F32),
-                pltpu.VMEM((span, heads * tokens), BF16),
-                pltpu.VMEM((span, heads * tokens), BF16),
+                pltpu.VMEM((span, lanes), F32),
+                pltpu.VMEM((span, lanes), F32),
+                pltpu.VMEM((span, queries), BF16),
+                pltpu.VMEM((span, queries), BF16),
                 pltpu.VMEM(qc.shape, BF16),
                 pltpu.VMEM(gl.shape, BF16),
                 pltpu.SemaphoreType.DMA((2,)),
             ],
         ),
-        compiler_params=pltpu.CompilerParams(vmem_limit_bytes=36 << 20),
+        compiler_params=pltpu.CompilerParams(vmem_limit_bytes=38 << 20),
         cost_estimate=pl.CostEstimate(
-            flops=2 * heads * tokens * span * (2 * width + 2 * latw),
-            transcendentals=heads * tokens * span, bytes_accessed=24 << 20,
+            flops=4 * queries * span * (width + latw),
+            transcendentals=queries * span, bytes_accessed=24 << 20,
         ),
         name="attend",
     )(info, doc_start, qct, glt, bias, own, *mine, *theirs, qc, gl)
@@ -252,17 +253,18 @@
             join(keys_s.at[:, pl.ds(block * tokens, tokens)], core, mine, theirs)
         keys_s[:, BACK * tokens :] = own_ref[...]
 
+    all_dq = dot(keys_s[...], ds_ref[...]) * factor
     for n in range(pair):
-        dq = dot(keys_s[...], ds_ref[n]) * factor
+        dq = all_dq[:, n * tokens : (n + 1) * tokens]
         dq_nope = dot(uk_ref[n], dq[:latw].astype(BF16), ((0,), (0,)))
         out_ref[n, :nope] = dq_nope.astype(BF16)
         out_ref[n, nope:] = dq[latw:].astype(BF16)
 
 
-def query_gradient(info, ds, w_uk, own, mine, theirs, factor, pair=2):
-    heads, span, tokens = ds.shape
-    latw, nope = w_uk.shape[1:]
-    width = own.shape[0]
+def query_gradient(info, ds, w_uk, own, mine, theirs, factor, pair=4):
+    span = ds.shape[0]
+    heads, latw, nope = w_uk.shape
+    width, tokens = own.shape
     qw = nope + width - latw
     whole = lambda a: pl.BlockSpec(a.shape, lambda h, s: (0,) * a.ndim)
     return pl.pallas_call(
@@ -272,7 +274,7 @@
             num_scalar_prefetch=1,
             grid=(heads // pair,),
             in_specs=[
-                pl.BlockSpec((pair, span, tokens), lambda h, s: (h, 0, 0)),
+                pl.BlockSpec((span, pair * tokens), lambda h, s: (0, h)),
                 pl.BlockSpec((pair, latw, nope), lambda h, s: (h, 0, 0)),
                 whole(own),
             ]
@@ -280,7 +282,7 @@
             out_specs=pl.BlockSpec((pair, qw, tokens), lambda h, s: (h, 0, 0)),
             scratch_shapes=[pltpu.VMEM((width, span), BF16)],
         ),
-        compiler_params=pltpu.CompilerParams(vmem_limit_bytes=16 << 20),
+        compiler_params=pltpu.CompilerParams(vmem_limit_bytes=24 << 20),
         cost_estimate=pl.CostEstimate(
             flops=2 * heads * tokens * (span * width + latw * nope),
             transcendentals=0, bytes_accessed=8 << 20,
@@ -301,13 +303,13 @@
     return pairs
 
 
-def between(source, target, mirrored=False):
+def between(source, target, turned=False):
     heads = lax.axis_size("head")
     pairs = []
     for head in range(heads):
         chip, core = divmod(head, CORES)
-        if mirrored:
-            chip = heads // CORES - 1 - chip
+        if turned:
+            chip ^= heads // CORES // 2
         pairs.append((source * heads + head, target * heads + chip * CORES + core))
     return pairs
 
@@ -341,7 +343,6 @@
     middle = lax.axis_size("seq") // 2
     after, next_one, next_two = middle, middle + 1, middle + 2
     relays = (between(next_one, after) + between(next_two, next_one), between(next_two, after))
-    returns = (between(after, next_one) + between(next_one, next_two), between(after, next_two))
 
     info = jnp.stack([core, (seq - BACK) * tokens]).astype(jnp.int32)
     qt = jnp.transpose(queries, (1, 2, 0))
@@ -359,34 +360,40 @@
     ds, keep, away = attend(
         info, doc_start, qct, glt, bias, own, mine, theirs, qc, gl, factor, chips
     )
-    arrived = swap_cores(away)
-    far, *near, total = list(keep + arrived)
-    for piece, route in zip(near, returns):
-        far = far + send(piece, route)
-    far, near = lax.optimization_barrier((far, near))
-    back = [send(piece, along_seq(-distance, False)) for piece, distance in zip(near, (2, 1))]
-    back.append(send(far, along_seq(-3)))
+    both = keep + swap_cores(away)
+    kept, gone = halve(both, 1, chip, 1)
+    both = kept.astype(F32) + trade(gone, 1).astype(F32)
+    *far, total = list(both)
+    back = [
+        send(far[BACK - distance].astype(BF16), along_seq(-distance))
+        for distance in range(1, BACK + 1)
+    ]
     dq = query_gradient(info, in_hbm(ds), in_hbm(w_uk), own, mine, theirs, factor)
-    back, dq = lax.optimization_barrier((back[::-1], dq))
-    total = total.astype(F32)
+    back, dq = lax.optimization_barrier((back, dq))
     for piece in back:
         total = total + piece.astype(F32)
+    bit = 2
+    while bit < chips:
+        kept, gone = halve(total, 0, chip, bit)
+        total = kept + trade(gone.astype(BF16), bit).astype(F32)
+        bit *= 2
     grad_query = jnp.transpose(dq, (2, 0, 1))
-    return grad_query, scatter_sum(total, chip)
-
-
-def scatter_sum(total, chip):
-    chips, rows, width = total.shape
-    bit = 1
-    while bit < chips:
-        mine = chip // bit % 2
-        halves = total.reshape(-1, 2, rows, width)
-        away = lax.dynamic_index_in_dim(halves, 1 - mine, 1, False).astype(BF16)
-        route = [(k, k ^ (bit * CORES)) for k in range(chips * CORES)]
-        arrived = lax.ppermute(away, "head", route)
-        total = lax.dynamic_index_in_dim(halves, mine, 1, False) + arrived.astype(F32)
-        bit *= 2
-    return total[0]
+    return grad_query, total[0]
+
+
+def halve(value, dim, chip, bit):
+    lengths = value.shape
+    halves = value.reshape(*lengths[:dim], lengths[dim] // 2, 2, *lengths[dim + 1 :])
+    mine = chip // bit % 2
+    return (
+        lax.dynamic_index_in_dim(halves, mine, dim + 1, False),
+        lax.dynamic_index_in_dim(halves, 1 - mine, dim + 1, False),
+    )
+
+
+def trade(value, bit):
+    route = [(k, k ^ (bit * CORES)) for k in range(lax.axis_size("head"))]
+    return lax.ppermute(value, "head", route)
 
 
 def solution(mesh):

time: 87.1 us -> 80.1 us (0.920)
  the two profiles are of different devices: /device:TPU:132 before, /device:TPU:62 now
where the time goes in v1:
time: 80.1 us; the launch traced here: 80.4 us
  Pallas kernels  29.2 us (36%)
  starting transfers between devices  26.7 us (33%)
  waiting for transfers between devices  20.2 us (25%)
  local copies, waits for them, and re-layouts  2.34 us (3%)
  other arithmetic  1.11 us (1%)
  between operations  0.87 us (1%)
    ppermute x8, starting transfers between devices, send(): return lax.ppermute(value, ('seq', 'head'), pairs)  21.7 us
    pallas_call x1, Pallas kernels, attend(): pl.pallas_call(functools.partial(main_kernel, factor=factor), out_shape=(...  17.8 us
    ppermute x2, waiting for transfers between devices, trade(): return lax.ppermute(value, 'head', route)  12.3 us
    pallas_call x1, Pallas kernels, query_gradient(): pl.pallas_call(functools.partial(query_kernel, factor=factor), out_shape=...  6.22 us
    pallas_call x1, Pallas kernels, prepare(): pl.pallas_call(prepare_kernel, out_shape=(jax.ShapeDtypeStruct((width, he...  5.24 us
    ppermute x8, waiting for transfers between devices, send(): return lax.ppermute(value, ('seq', 'head'), pairs)  4.56 us
    ppermute x2, starting transfers between devices, trade(): return lax.ppermute(value, 'head', route)  4.04 us
    ppermute x4, waiting for transfers between devices, swap_cores(): lax.ppermute(value, 'head', [(k, k ^ 1) for k in range(lax.axis_size('hea...  3.29 us
  transfers between devices with their start and end apart: 14, of which 7 were waited for; matrix products, arithmetic and copies ran while one was open for 2% of the time, Pallas kernels for 14%

profile of v1, /device:TPU:62, one launch (start us, length us, event | category | flops | bytes accessed | tf_op | source)
XLA Modules:
  0.0 80.4 jit_solution(17845846831699778873)
XLA Ops:
  0.6 0.9 %dynamic-slice_bitcast_fusion.1 = bf16[288,256]{1,0:T(8,128)(2,1)S(1)} fusion(bf16[256,576]{0,1:T(8,128)(2,1)} %param.8, s32[]{:T(128)S(6)} %select_n.41), kind=kLoop, calls=%fused_computation.6 | loop fusion | bytes 294916 | tf_op jit(solution)/shard_map/dynamic_slice | solution.py:339
  1.6 7.4 %collective-permute-start.2 = (bf16[288,256]{1,0:T(8,128)(2,1)S(1)}, bf16[288,256]{1,0:T(8,128)(2,1)S(1)}, u32[]{:S(2)}, u32[]{:S(2)}) collective-permute-start(bf16[288,256]{1,0:T(8,128)(2,1)S(1)} %dynamic-slice_bitcast_fusion.1), channel_id=1, source_target_pairs={{0,24},{1,25},{2,26},{3,27},{4,28},{5,29},{6,30},{7,31},{8,32},{9,... | collective-permute-start | bytes 442376 | tf_op jit(solution)/shard_map/ppermute | solution.py:318
  9.0 1.3 %collective-permute-start.1 = (bf16[288,256]{1,0:T(8,128)(2,1)S(1)}, bf16[288,256]{1,0:T(8,128)(2,1)S(1)}, u32[]{:S(2)}, u32[]{:S(2)}) collective-permute-start(bf16[288,256]{1,0:T(8,128)(2,1)S(1)} %dynamic-slice_bitcast_fusion.1), channel_id=1, source_target_pairs={{0,16},{1,17},{2,18},{3,19},{4,20},{5,21},{6,22},{7,23},{8,24},{9,... | collective-permute-start | bytes 442376 | tf_op jit(solution)/shard_map/ppermute | solution.py:318
  10.3 1.3 %collective-permute-start = (bf16[288,256]{1,0:T(8,128)(2,1)S(1)}, bf16[288,256]{1,0:T(8,128)(2,1)S(1)}, u32[]{:S(2)}, u32[]{:S(2)}) collective-permute-start(bf16[288,256]{1,0:T(8,128)(2,1)S(1)} %dynamic-slice_bitcast_fusion.1), channel_id=1, source_target_pairs={{0,8},{1,9},{2,10},{3,11},{4,12},{5,13},{6,14},{7,15},{8,16},{9,17... | collective-permute-start | bytes 442376 | tf_op jit(solution)/shard_map/ppermute | solution.py:318
  11.6 1.3 %copy.8 = bf16[256,8,128]{0,2,1:T(8,128)(2,1)S(1)} copy(bf16[256,8,128]{2,1,0:T(8,128)(2,1)} %param.7) | data formatting | bytes 1048576 | tf_op args[1]
  12.9 0.0 collective-permute-done.2.m3_ref
  12.9 0.7 collective-permute-start.4
  13.6 0.7 collective-permute-start.3
  14.3 0.1 pad_add_fusion.info_ref
  14.4 0.0 collective-permute-start.5
  14.4 0.0 copy-start
  14.4 0.0 copy-start.1
  14.4 5.2 %prepare.1 = (bf16[576,2048]{1,0:T(8,128)(2,1)S(1)}, bf16[2048,576]{1,0:T(8,128)(2,1)S(1)}, bf16[512,2048]{1,0:T(8,128)(2,1)S(1)}, bf16[2048,512]{1,0:T(8,128)(2,1)S(1)}, f32[1024,256]{1,0:T(8,128)S(1)}) custom-call(s32[2]{0:T(128)S(1)} %pad_add_fusion.info_ref, bf16[8,192,256]{2,1,0:T(8,128)(2,1)} %bitcast.40, bf16[8,128,256]{2,1,0:T(8,128)(2,1)S(1)} %bitcast.34, ...), custom_call_target="tpu_custom_call" | custom-call | flops 1073741824 | bytes 16777216 | tf_op jit(solution)/shard_map/prepare/pallas_call | solution.py:58
  19.7 0.0 collective-permute-done.1
  19.7 0.0 collective-permute-done
  19.7 0.0 collective-permute-done.4
  19.7 0.0 collective-permute-done.3
  19.8 0.6 collective-permute-start.7
  20.4 0.1 collective-permute-start.6
  20.5 0.0 collective-permute-done.5.t3_ref
  20.5 0.8 %collective-permute-done.7.t1_ref = bf16[288,256]{1,0:T(8,128)(2,1)S(1)} collective-permute-done((bf16[288,256]{1,0:T(8,128)(2,1)S(1)}, bf16[288,256]{1,0:T(8,128)(2,1)S(1)}, u32[]{:S(2)}, u32[]{:S(2)}) %collective-permute-start.7) | collective-permute-done | bytes 147488 | tf_op jit(solution)/shard_map/ppermute | solution.py:326
  21.3 0.5 collective-permute-done.6.t2_ref
  21.8 0.0 copy-done
  21.8 0.0 copy-done.1
  21.8 17.8 %attend.1 = (bf16[1024,2048]{1,0:T(8,128)(2,1)}, bf16[4,4,32,576]{3,2,1,0:T(8,128)(2,1)S(1)}, bf16[4,4,32,576]{3,2,1,0:T(8,128)(2,1)S(1)}) custom-call(s32[2]{0:T(128)S(1)} %pad_add_fusion.info_ref, s32[256]{0:T(256)S(1)} %copy-done.1, bf16[576,2048]{1,0:T(8,128)(2,1)S(1)} %get-tuple-element.32.qct_ref, bf16[512,2048]{1,0:T(8,128)(2,1)S(1)} %get-tuple-element.33.glt_ref, ...), custom_call_target="tpu_custom_call" | custom-call | flops 9126805504 | bytes 25165824 | tf_op jit(solution)/shard_map/attend/pallas_call | solution.py:201
  39.6 0.2 collective-permute-start.8
  39.9 2.0 %collective-permute-done.8 = bf16[4,4,32,576]{3,2,1,0:T(8,128)(2,1)S(1)} collective-permute-done((bf16[4,4,32,576]{3,2,1,0:T(8,128)(2,1)S(1)}, bf16[4,4,32,576]{3,2,1,0:T(8,128)(2,1)S(1)}, u32[]{:S(2)}, u32[]{:S(2)}) %collective-permute-start.8) | collective-permute-done | bytes 589856 | tf_op jit(solution)/shard_map/ppermute | solution.py:326
  41.8 0.2 add.61
  42.0 3.4 %collective-permute-start.9 = (bf16[4,2,32,576]{3,2,1,0:T(8,128)(2,1)S(1)}, bf16[4,2,32,576]{3,2,1,0:T(8,128)(2,1)S(1)}, u32[]{:S(2)}, u32[]{:S(2)}) collective-permute-start(bf16[4,2,32,576]{3,2,1,0:T(8,128)(2,1)S(1)} %dynamic-slice_bitcast_fusion), channel_id=1, source_target_pairs={{0,2},{1,3},{2,0},{3,1},{4,6},{5,7},{6,4},{7,5},{8,10},{9,11},{10,... | collective-permute-start | bytes 884744 | tf_op jit(solution)/shard_map/ppermute | solution.py:396
  45.4 8.0 %collective-permute-done.9 = bf16[4,2,32,576]{3,2,1,0:T(8,128)(2,1)S(1)} collective-permute-done((bf16[4,2,32,576]{3,2,1,0:T(8,128)(2,1)S(1)}, bf16[4,2,32,576]{3,2,1,0:T(8,128)(2,1)S(1)}, u32[]{:S(2)}, u32[]{:S(2)}) %collective-permute-start.9) | collective-permute-done | bytes 294944 | tf_op jit(solution)/shard_map/ppermute | solution.py:396
  53.4 0.1 fusion.3
  53.6 5.7 %collective-permute-start.12 = (bf16[2,32,576]{2,1,0:T(8,128)(2,1)S(1)}, bf16[2,32,576]{2,1,0:T(8,128)(2,1)S(1)}, u32[]{:S(2)}, u32[]{:S(2)}) collective-permute-start(bf16[2,32,576]{2,1,0:T(8,128)(2,1)S(1)} %get-tuple-element.50), channel_id=1, source_target_pairs={{24,0},{25,1},{26,2},{27,3},{28,4},{29,5},{30,6},{31,7},{32,8},{33... | collective-permute-start | bytes 221192 | tf_op jit(solution)/shard_map/ppermute | solution.py:318
  59.3 1.9 %collective-permute-start.11 = (bf16[2,32,576]{2,1,0:T(8,128)(2,1)S(1)}, bf16[2,32,576]{2,1,0:T(8,128)(2,1)S(1)}, u32[]{:S(2)}, u32[]{:S(2)}) collective-permute-start(bf16[2,32,576]{2,1,0:T(8,128)(2,1)S(1)} %get-tuple-element.51), channel_id=1, source_target_pairs={{16,0},{17,1},{18,2},{19,3},{20,4},{21,5},{22,6},{23,7},{24,8},{25... | collective-permute-start | bytes 221192 | tf_op jit(solution)/shard_map/ppermute | solution.py:318
  61.2 2.8 %collective-permute-start.10 = (bf16[2,32,576]{2,1,0:T(8,128)(2,1)S(1)}, bf16[2,32,576]{2,1,0:T(8,128)(2,1)S(1)}, u32[]{:S(2)}, u32[]{:S(2)}) collective-permute-start(bf16[2,32,576]{2,1,0:T(8,128)(2,1)S(1)} %get-tuple-element.52), channel_id=1, source_target_pairs={{8,0},{9,1},{10,2},{11,3},{12,4},{13,5},{14,6},{15,7},{16,8},{17,9... | collective-permute-start | bytes 221192 | tf_op jit(solution)/shard_map/ppermute | solution.py:318
  64.0 6.2 %query_gradient.1 = bf16[8,192,256]{2,1,0:T(8,128)(2,1)} custom-call(s32[2]{0:T(128)S(1)} %pad_add_fusion.info_ref, bf16[1024,2048]{1,0:T(8,128)(2,1)} %get-tuple-element.43.ds_ref, bf16[8,512,128]{2,1,0:T(8,128)(2,1)} %uk_ref.3, bf16[576,256]{1,0:T(8,128)(2,1)S(1)} %bitcast.36, bf16[288,256]{1,0:T(8,128)(2,1)S(1)} %collective-permute-done.2.m3_ref, ...), custom_call_target="tpu_custom_call" | custom-call | flops 2684354560 | bytes 8388608 | tf_op jit(solution)/shard_map/query_gradient/pallas_call | solution.py:270
  70.2 0.0 collective-permute-done.12
  70.2 3.2 %collective-permute-done.11 = bf16[2,32,576]{2,1,0:T(8,128)(2,1)S(1)} collective-permute-done((bf16[2,32,576]{2,1,0:T(8,128)(2,1)S(1)}, bf16[2,32,576]{2,1,0:T(8,128)(2,1)S(1)}, u32[]{:S(2)}, u32[]{:S(2)}) %collective-permute-start.11) | collective-permute-done | bytes 73760 | tf_op jit(solution)/shard_map/ppermute | solution.py:318
  73.4 1.4 %collective-permute-done.10 = bf16[2,32,576]{2,1,0:T(8,128)(2,1)S(1)} collective-permute-done((bf16[2,32,576]{2,1,0:T(8,128)(2,1)S(1)}, bf16[2,32,576]{2,1,0:T(8,128)(2,1)S(1)}, u32[]{:S(2)}, u32[]{:S(2)}) %collective-permute-start.10) | collective-permute-done | bytes 73760 | tf_op jit(solution)/shard_map/ppermute | solution.py:318
  74.8 0.7 collective-permute-start.13
  75.5 4.3 %collective-permute-done.13 = bf16[1,32,576]{2,1,0:T(8,128)(2,1)S(1)} collective-permute-done((bf16[1,32,576]{2,1,0:T(8,128)(2,1)S(1)}, bf16[1,32,576]{2,1,0:T(8,128)(2,1)S(1)}, u32[]{:S(2)}, u32[]{:S(2)}) %collective-permute-start.13) | collective-permute-done | bytes 36896 | tf_op jit(solution)/shard_map/ppermute | solution.py:396
  79.8 0.6 add_bitcast_fusion
  (6 shorter events, 0.2 us)
Async XLA Ops:
  1.6 11.3 %collective-permute-start.2 = (bf16[288,256]{1,0:T(8,128)(2,1)S(1)}, bf16[288,256]{1,0:T(8,128)(2,1)S(1)}, u32[]{:S(2)}, u32[]{:S(2)}) collective-permute-start(bf16[288,256]{1,0:T(8,128)(2,1)S(1)} %dynamic-slice_bitcast_fusion.1), channel_id=1, source_target_pairs={{0,24},{1,25},{2,26},{3,27},{4,28},{5,29},{6,30},{7,31},{8,32},{9,... | collective-permute-start | bytes 442376 | tf_op jit(solution)/shard_map/ppermute | solution.py:318
  9.0 10.7 %collective-permute-start.1 = (bf16[288,256]{1,0:T(8,128)(2,1)S(1)}, bf16[288,256]{1,0:T(8,128)(2,1)S(1)}, u32[]{:S(2)}, u32[]{:S(2)}) collective-permute-start(bf16[288,256]{1,0:T(8,128)(2,1)S(1)} %dynamic-slice_bitcast_fusion.1), channel_id=1, source_target_pairs={{0,16},{1,17},{2,18},{3,19},{4,20},{5,21},{6,22},{7,23},{8,24},{9,... | collective-permute-start | bytes 442376 | tf_op jit(solution)/shard_map/ppermute | solution.py:318
  10.3 9.4 %collective-permute-start = (bf16[288,256]{1,0:T(8,128)(2,1)S(1)}, bf16[288,256]{1,0:T(8,128)(2,1)S(1)}, u32[]{:S(2)}, u32[]{:S(2)}) collective-permute-start(bf16[288,256]{1,0:T(8,128)(2,1)S(1)} %dynamic-slice_bitcast_fusion.1), channel_id=1, source_target_pairs={{0,8},{1,9},{2,10},{3,11},{4,12},{5,13},{6,14},{7,15},{8,16},{9,17... | collective-permute-start | bytes 442376 | tf_op jit(solution)/shard_map/ppermute | solution.py:318
  12.9 6.8 %collective-permute-start.4 = (bf16[288,256]{1,0:T(8,128)(2,1)S(1)}, bf16[288,256]{1,0:T(8,128)(2,1)S(1)}, u32[]{:S(2)}, u32[]{:S(2)}) collective-permute-start(bf16[288,256]{1,0:T(8,128)(2,1)S(1)} %collective-permute-done.2.m3_ref), channel_id=1, source_target_pairs={{144,128},{145,129},{146,130},{147,131},{148,132},{149,133},{150,1... | collective-permute-start | bytes 442376 | tf_op jit(solution)/shard_map/ppermute | solution.py:318
  13.6 6.1 %collective-permute-start.3 = (bf16[288,256]{1,0:T(8,128)(2,1)S(1)}, bf16[288,256]{1,0:T(8,128)(2,1)S(1)}, u32[]{:S(2)}, u32[]{:S(2)}) collective-permute-start(bf16[288,256]{1,0:T(8,128)(2,1)S(1)} %collective-permute-done.2.m3_ref), channel_id=1, source_target_pairs={{136,128},{137,129},{138,130},{139,131},{140,132},{141,133},{142,1... | collective-permute-start | bytes 442376 | tf_op jit(solution)/shard_map/ppermute | solution.py:318
  14.4 6.1 %collective-permute-start.5 = (bf16[288,256]{1,0:T(8,128)(2,1)S(1)}, bf16[288,256]{1,0:T(8,128)(2,1)S(1)}, u32[]{:S(2)}, u32[]{:S(2)}) collective-permute-start(bf16[288,256]{1,0:T(8,128)(2,1)S(1)} %collective-permute-done.2.m3_ref), channel_id=1, source_target_pairs={{0,1},{1,0},{2,3},{3,2},{4,5},{5,4},{6,7},{7,6},{8,9},{9,8},{10,11... | collective-permute-start | bytes 442376 | tf_op jit(solution)/shard_map/ppermute | solution.py:326
  14.4 7.4 %copy-start = (bf16[256,576]{0,1:T(8,128)(2,1)S(1)}, bf16[256,576]{0,1:T(8,128)(2,1)}, u32[]{:S(2)}) copy-start(bf16[256,576]{0,1:T(8,128)(2,1)} %param.8) | copy-start | bytes 884740
  14.4 7.4 %copy-start.1 = (s32[256]{0:T(256)S(1)}, s32[256]{0:T(256)}, u32[]{:S(2)}) copy-start(s32[256]{0:T(256)} %start_ref.1) | copy-start | bytes 3076
  19.8 1.6 %collective-permute-start.7 = (bf16[288,256]{1,0:T(8,128)(2,1)S(1)}, bf16[288,256]{1,0:T(8,128)(2,1)S(1)}, u32[]{:S(2)}, u32[]{:S(2)}) collective-permute-start(bf16[288,256]{1,0:T(8,128)(2,1)S(1)} %add.60.m1_ref), channel_id=1, source_target_pairs={{0,1},{1,0},{2,3},{3,2},{4,5},{5,4},{6,7},{7,6},{8,9},{9,8},{10,11... | collective-permute-start | bytes 442376 | tf_op jit(solution)/shard_map/ppermute | solution.py:326
  20.4 1.5 %collective-permute-start.6 = (bf16[288,256]{1,0:T(8,128)(2,1)S(1)}, bf16[288,256]{1,0:T(8,128)(2,1)S(1)}, u32[]{:S(2)}, u32[]{:S(2)}) collective-permute-start(bf16[288,256]{1,0:T(8,128)(2,1)S(1)} %add.59.m2_ref), channel_id=1, source_target_pairs={{0,1},{1,0},{2,3},{3,2},{4,5},{5,4},{6,7},{7,6},{8,9},{9,8},{10,11... | collective-permute-start | bytes 442376 | tf_op jit(solution)/shard_map/ppermute | solution.py:326
  39.6 2.2 %collective-permute-start.8 = (bf16[4,4,32,576]{3,2,1,0:T(8,128)(2,1)S(1)}, bf16[4,4,32,576]{3,2,1,0:T(8,128)(2,1)S(1)}, u32[]{:S(2)}, u32[]{:S(2)}) collective-permute-start(bf16[4,4,32,576]{3,2,1,0:T(8,128)(2,1)S(1)} %get-tuple-element.42), channel_id=1, source_target_pairs={{0,1},{1,0},{2,3},{3,2},{4,5},{5,4},{6,7},{7,6},{8,9},{9,8},{10,11... | collective-permute-start | bytes 1769480 | tf_op jit(solution)/shard_map/ppermute | solution.py:326
  42.0 11.4 %collective-permute-start.9 = (bf16[4,2,32,576]{3,2,1,0:T(8,128)(2,1)S(1)}, bf16[4,2,32,576]{3,2,1,0:T(8,128)(2,1)S(1)}, u32[]{:S(2)}, u32[]{:S(2)}) collective-permute-start(bf16[4,2,32,576]{3,2,1,0:T(8,128)(2,1)S(1)} %dynamic-slice_bitcast_fusion), channel_id=1, source_target_pairs={{0,2},{1,3},{2,0},{3,1},{4,6},{5,7},{6,4},{7,5},{8,10},{9,11},{10,... | collective-permute-start | bytes 884744 | tf_op jit(solution)/shard_map/ppermute | solution.py:396
  53.6 16.6 %collective-permute-start.12 = (bf16[2,32,576]{2,1,0:T(8,128)(2,1)S(1)}, bf16[2,32,576]{2,1,0:T(8,128)(2,1)S(1)}, u32[]{:S(2)}, u32[]{:S(2)}) collective-permute-start(bf16[2,32,576]{2,1,0:T(8,128)(2,1)S(1)} %get-tuple-element.50), channel_id=1, source_target_pairs={{24,0},{25,1},{26,2},{27,3},{28,4},{29,5},{30,6},{31,7},{32,8},{33... | collective-permute-start | bytes 221192 | tf_op jit(solution)/shard_map/ppermute | solution.py:318
  59.3 14.1 %collective-permute-start.11 = (bf16[2,32,576]{2,1,0:T(8,128)(2,1)S(1)}, bf16[2,32,576]{2,1,0:T(8,128)(2,1)S(1)}, u32[]{:S(2)}, u32[]{:S(2)}) collective-permute-start(bf16[2,32,576]{2,1,0:T(8,128)(2,1)S(1)} %get-tuple-element.51), channel_id=1, source_target_pairs={{16,0},{17,1},{18,2},{19,3},{20,4},{21,5},{22,6},{23,7},{24,8},{25... | collective-permute-start | bytes 221192 | tf_op jit(solution)/shard_map/ppermute | solution.py:318
  61.2 13.5 %collective-permute-start.10 = (bf16[2,32,576]{2,1,0:T(8,128)(2,1)S(1)}, bf16[2,32,576]{2,1,0:T(8,128)(2,1)S(1)}, u32[]{:S(2)}, u32[]{:S(2)}) collective-permute-start(bf16[2,32,576]{2,1,0:T(8,128)(2,1)S(1)} %get-tuple-element.52), channel_id=1, source_target_pairs={{8,0},{9,1},{10,2},{11,3},{12,4},{13,5},{14,6},{15,7},{16,8},{17,9... | collective-permute-start | bytes 221192 | tf_op jit(solution)/shard_map/ppermute | solution.py:318
  74.8 5.0 %collective-permute-start.13 = (bf16[1,32,576]{2,1,0:T(8,128)(2,1)S(1)}, bf16[1,32,576]{2,1,0:T(8,128)(2,1)S(1)}, u32[]{:S(2)}, u32[]{:S(2)}) collective-permute-start(bf16[1,32,576]{2,1,0:T(8,128)(2,1)S(1)} %dynamic-slice_convert_fusion), channel_id=1, source_target_pairs={{0,4},{1,5},{2,6},{3,7},{4,0},{5,1},{6,2},{7,3},{8,12},{9,13},{10,... | collective-permute-start | bytes 110600 | tf_op jit(solution)/shard_map/ppermute | solution.py:396
